TPU v7x, 32 devices: a whole 2x2x4 slice. The times are simulated.
32 devices in a mesh: cand: 4 (over x, core), seq: 8 (over z, y).
Axes of the slice: x: 2, y: 2, z: 4, core: 2. Of those that a mesh axis runs over, the one named last changes fastest.
Arguments:
- response_query_array: bfloat16 [8, 768, 2560], P('cand', 'seq'), may hold values from -180 to 180
- response_key_array: bfloat16 [8, 768, 512], P('cand', 'seq'), may hold values from -6 to 6
- response_value_array: bfloat16 [8, 768, 512], P('cand', 'seq'), may hold values from -6 to 6
- prompt_key_array: bfloat16 [2048, 512], P(('cand', 'seq')), may hold values from -6 to 6
- prompt_value_array: bfloat16 [2048, 512], P(('cand', 'seq')), may hold values from -6 to 6
- lengths: int32 [8], replicated, may hold values from 192 to 768, as said below
- offsets: int32 [8], replicated, may hold values from 512 to 2048, as said below
- ranks: int32 [8], replicated, may hold values from 0 to 7, each once
Outputs:
- attention: bfloat16 [8, 768, 2560], P('cand', 'seq')
Inputs may be any that keep to these rules, and one draw needn't show every extreme that they name: `lengths`: some candidate's response has all 768 positions live. `offsets`: some candidate sees the whole prompt.
All inputs are finite; a program needn't handle non-finite values.
Results may differ from a plain program's by a relative error of at most 0.004.
Values may be sent and summed in bfloat16 or wider, within the bound.
No kernel may reach another device: no remote copies, remote signals or barrier semaphores. Data moves between devices by JAX's collectives and lax.ppermute only.
A program may use at most 128 MiB of HBM per device.

v0:
```python
import math
import jax
import jax.numpy as jnp
from jax import lax
from jax.sharding import PartitionSpec as P

QUERY_HEADS = 20
KEY_VALUE_HEADS = 4
HEAD_DIMENSION = 128
lowest_score_value = -1e30


def attend_block(running, query_rows, block_keys, block_values, allowed, shared):
    running_max, running_total, running_sum = running
    cand_count = query_rows.shape[0]
    heads_kv = query_rows.shape[2]
    head_size = query_rows.shape[4]
    score_scale = 1.0 / math.sqrt(head_size)
    if shared:
        keys_split = block_keys.reshape(block_keys.shape[0], heads_kv, head_size)
        values_split = block_values.reshape(block_values.shape[0], heads_kv, head_size)
        scores = jnp.einsum(
            "crhgd,nhd->chgrn", query_rows, keys_split, preferred_element_type=jnp.float32
        )
    else:
        keys_split = block_keys.reshape(cand_count, block_keys.shape[1], heads_kv, head_size)
        values_split = block_values.reshape(cand_count, block_values.shape[1], heads_kv, head_size)
        scores = jnp.einsum(
            "crhgd,cnhd->chgrn", query_rows, keys_split, preferred_element_type=jnp.float32
        )
    scores = jnp.where(allowed[:, None, None, :, :], scores * score_scale, -jnp.inf)
    new_max = jnp.maximum(running_max, jnp.max(scores, axis=-1))
    rescale = jnp.exp(running_max - new_max)
    exponent = jnp.exp(scores - new_max[..., None])
    weights = exponent.astype(jnp.bfloat16)
    new_total = running_total * rescale + jnp.sum(exponent, axis=-1)
    if shared:
        contrib = jnp.einsum(
            "chgrn,nhd->chgrd", weights, values_split, preferred_element_type=jnp.float32
        )
    else:
        contrib = jnp.einsum(
            "chgrn,cnhd->chgrd", weights, values_split, preferred_element_type=jnp.float32
        )
    new_sum = running_sum * rescale[..., None] + contrib
    return (new_max, new_total, new_sum)


def fold_blocks(
    running, query_rows, all_keys, all_values, key_pos, allowed_of, shared, live_of=None
):
    key_count = key_pos.shape[0]
    block_len = math.gcd(key_count, 512)
    keys_axis = 0 if shared else 1

    def one_block(step_at, carried):
        block_start = step_at * block_len
        block_keys = lax.dynamic_slice_in_dim(all_keys, block_start, block_len, keys_axis)
        block_values = lax.dynamic_slice_in_dim(all_values, block_start, block_len, keys_axis)
        block_pos = lax.dynamic_slice_in_dim(key_pos, block_start, block_len, 0)
        return attend_block(
            carried, query_rows, block_keys, block_values, allowed_of(block_pos), shared
        )

    return lax.fori_loop(0, key_count // block_len, one_block, running)


def body(
    response_query_array,
    response_key_array,
    response_value_array,
    prompt_key_array,
    prompt_value_array,
    lengths,
    offsets,
    ranks,
):
    candidate_local, output_rows, width = response_query_array.shape
    group_width = QUERY_HEADS // KEY_VALUE_HEADS
    group_at = lax.axis_index("cand")
    seq_at = lax.axis_index("seq")
    first_cand = group_at * candidate_local
    my_lengths = lax.dynamic_slice_in_dim(lengths, first_cand, candidate_local)
    my_offsets = lax.dynamic_slice_in_dim(offsets, first_cand, candidate_local)
    query_pos = seq_at * output_rows + jnp.arange(output_rows, dtype=jnp.int32)
    query_rows = response_query_array.reshape(
        candidate_local, output_rows, KEY_VALUE_HEADS, group_width, HEAD_DIMENSION
    )
    pieces = (
        lax.all_gather(prompt_key_array, ("cand", "seq"), axis=0, tiled=True),
        lax.all_gather(prompt_value_array, ("cand", "seq"), axis=0, tiled=True),
    )
    key_pos = jnp.arange(pieces[0].shape[0], dtype=jnp.int32)

    def allowed_of(block_pos):
        return block_pos[None, None, :] < my_offsets[:, None, None]

    running = fold_blocks(
        (
            jnp.full(
                (candidate_local, KEY_VALUE_HEADS, group_width, output_rows),
                lowest_score_value,
                jnp.float32,
            ),
            jnp.zeros((candidate_local, KEY_VALUE_HEADS, group_width, output_rows), jnp.float32),
            jnp.zeros(
                (candidate_local, KEY_VALUE_HEADS, group_width, output_rows, HEAD_DIMENSION),
                jnp.float32,
            ),
        ),
        query_rows,
        pieces[0],
        pieces[1],
        key_pos,
        allowed_of,
        True,
    )
    pieces = (
        lax.all_gather(response_key_array, "seq", axis=1, tiled=True),
        lax.all_gather(response_value_array, "seq", axis=1, tiled=True),
    )
    key_pos = jnp.arange(pieces[0].shape[1], dtype=jnp.int32)

    def allowed_of(block_pos):
        causal = block_pos[None, None, :] <= query_pos[None, :, None]
        return causal & (block_pos[None, None, :] < my_lengths[:, None, None])

    final_max, final_total, final_sum = fold_blocks(
        running, query_rows, pieces[0], pieces[1], key_pos, allowed_of, False
    )
    attended = final_sum / final_total[..., None]
    attended = jnp.transpose(attended, (0, 3, 1, 2, 4)).reshape(candidate_local, output_rows, width)
    row_valid = query_pos[None, :] < my_lengths[:, None]
    attended = jnp.where(row_valid[:, :, None], attended, 0.0).astype(jnp.bfloat16)
    gathered = lax.all_gather(attended, "cand", axis=0, tiled=True)
    every_cand = jnp.arange(gathered.shape[0], dtype=jnp.int32)
    chosen = []
    for within in range(candidate_local):
        target = first_cand + within
        source = jnp.sum(jnp.where(ranks == target, every_cand, 0))
        chosen.append(lax.dynamic_index_in_dim(gathered, source, 0, keepdims=False))
    return jnp.stack(chosen, axis=0)


def solution(mesh):
    in_specs = (
        P("cand", "seq", None),
        P("cand", "seq", None),
        P("cand", "seq", None),
        P(("cand", "seq"), None),
        P(("cand", "seq"), None),
        P(),
        P(),
        P(),
    )
    out_specs = P("cand", "seq", None)
    return jax.shard_map(body, mesh=mesh, in_specs=in_specs, out_specs=out_specs, check_vma=False)
```

profile of v0, /device:TPU:0, one launch (start us, length us, event | category | flops | bytes accessed | tf_op | source)
XLA Modules:
  0.0 304.9 jit_solution(10088347945177968936)
XLA Ops:
  8.1 1.8 copy.56
  9.9 1.8 copy.57
  15.9 53.7 %all-gather.6.cloned.1.call-done = bf16[2048,512]{1,0:T(8,128)(2,1)} async-done(((bf16[64,512]{1,0:T(8,128)(2,1)}), bf16[2048,512]{1,0:T(8,128)(2,1)}) %all-gather.6.cloned.1.call-update) | async-done | bytes 2097168 | tf_op jit(solution)/shard_map/all_gather | solution.py:90
  69.6 58.4 %all-gather.8.cloned.1.call-done = bf16[2048,512]{1,0:T(8,128)(2,1)} async-done(((bf16[64,512]{1,0:T(8,128)(2,1)}), bf16[2048,512]{1,0:T(8,128)(2,1)}) %all-gather.8.cloned.1.call-update) | async-done | bytes 2097168 | tf_op jit(solution)/shard_map/all_gather | solution.py:91
  128.0 65.4 %while.37 = (s32[]{:T(128)}, f32[2,4,5,96]{3,2,0,1:T(8,128)S(1)}, f32[2,4,5,96]{3,2,0,1:T(8,128)S(1)}, f32[2,4,5,96,128]{4,3,2,0,1:T(8,128)}, s32[2048]{0:T(1024...) while((s32[]{:T(128)}, f32[2,4,5,96]{3,2,0,1:T(8,128)S(1)}, ...), condition=%wide.region_3.4_spmd.clone, body=%wide.region_0.3_spmd.clone.sunk | while | flops 1029754624 | bytes 34007236 | solution.py:65
  129.6 4.2 %fusion.60 = (f32[2,4,5,96]{3,2,0,1:T(8,128)S(1)}, f32[4,512,2,96,5]{1,3,4,2,0:T(8,128)}) fusion(pred[2,512]{1,0:T(4,128)(4,1)S(1)} %broadcast_compare_fusion.9, bf16[512,4,128,1,1]{0,2,4,3,1:T(8,128)(2,1)S(1)} %bitcast.88, bf16[2,96,4,5,128]{4,1,3,0,2:T(8,128)(2,1)S(1)} %get-tuple-element.683), kind=kOutput, calls=%fused_computation.26.clone.1 | convolution fusion | flops 509210880 | bytes 9388032 | tf_op jit(solution)/shard_map/while/body/eval_jaxpr/crhgd,nhd->chgrn/dot_general | solution.py:22
  133.9 4.5 %fusion.61 = f32[2,4,5,96]{3,2,0,1:T(8,128)S(1)} fusion(f32[4,512,2,96,5]{1,3,4,2,0:T(8,128)} %get-tuple-element.646, f32[2,4,5,96]{3,2,0,1:T(8,128)S(1)} %select_maximum_fusion.2, pred[2,512]{1,0:T(4,128)(4,1)S(1)} %broadcast_compare_fusion.9), kind=kLoop, calls=%fused_computation.25.clone.1 | loop fusion | flops 7860480 | bytes 7896064 | tf_op jit(solution)/shard_map/while/body/eval_jaxpr/reduce_sum | solution.py:36
  138.6 5.4 %bitcast_add_fusion.2 = f32[2,4,5,96,128]{4,3,2,0,1:T(8,128)} fusion(f32[2,4,5,96,128]{4,3,2,0,1:T(8,128)} %get-tuple-element.666, bf16[512,4,128,1,1]{0,2,4,3,1:T(8,128)(2,1)S(1)} %bitcast.91, f32[4,512,2,96,5]{1,3,4,2,0:T(8,128)} %get-tuple-element.646, f32[2,4,5,96]{3,2,0,1:T(8,128)S(1)} %select_maximum_fusion.2, ...), kind=kOutput, calls=%fused_computation.32.clone.1 | convolution fusion | flops 512655360 | bytes 12352513 | tf_op jit(solution)/shard_map/while/body/eval_jaxpr/chgrn,nhd->chgrd/dot_general | solution.py:38
  145.7 4.2 %fusion.60 = (f32[2,4,5,96]{3,2,0,1:T(8,128)S(1)}, f32[4,512,2,96,5]{1,3,4,2,0:T(8,128)}) fusion(pred[2,512]{1,0:T(4,128)(4,1)S(1)} %broadcast_compare_fusion.9, bf16[512,4,128,1,1]{0,2,4,3,1:T(8,128)(2,1)S(1)} %bitcast.88, bf16[2,96,4,5,128]{4,1,3,0,2:T(8,128)(2,1)S(1)} %get-tuple-element.683), kind=kOutput, calls=%fused_computation.26.clone.1 | convolution fusion | flops 509210880 | bytes 9388032 | tf_op jit(solution)/shard_map/while/body/eval_jaxpr/crhgd,nhd->chgrn/dot_general | solution.py:22
  149.9 4.4 %fusion.61 = f32[2,4,5,96]{3,2,0,1:T(8,128)S(1)} fusion(f32[4,512,2,96,5]{1,3,4,2,0:T(8,128)} %get-tuple-element.646, f32[2,4,5,96]{3,2,0,1:T(8,128)S(1)} %select_maximum_fusion.2, pred[2,512]{1,0:T(4,128)(4,1)S(1)} %broadcast_compare_fusion.9), kind=kLoop, calls=%fused_computation.25.clone.1 | loop fusion | flops 7860480 | bytes 7896064 | tf_op jit(solution)/shard_map/while/body/eval_jaxpr/reduce_sum | solution.py:36
  154.6 6.0 %bitcast_add_fusion.2 = f32[2,4,5,96,128]{4,3,2,0,1:T(8,128)} fusion(f32[2,4,5,96,128]{4,3,2,0,1:T(8,128)} %get-tuple-element.666, bf16[512,4,128,1,1]{0,2,4,3,1:T(8,128)(2,1)S(1)} %bitcast.91, f32[4,512,2,96,5]{1,3,4,2,0:T(8,128)} %get-tuple-element.646, f32[2,4,5,96]{3,2,0,1:T(8,128)S(1)} %select_maximum_fusion.2, ...), kind=kOutput, calls=%fused_computation.32.clone.1 | convolution fusion | flops 512655360 | bytes 12352513 | tf_op jit(solution)/shard_map/while/body/eval_jaxpr/chgrn,nhd->chgrd/dot_general | solution.py:38
  162.2 4.2 %fusion.60 = (f32[2,4,5,96]{3,2,0,1:T(8,128)S(1)}, f32[4,512,2,96,5]{1,3,4,2,0:T(8,128)}) fusion(pred[2,512]{1,0:T(4,128)(4,1)S(1)} %broadcast_compare_fusion.9, bf16[512,4,128,1,1]{0,2,4,3,1:T(8,128)(2,1)S(1)} %bitcast.88, bf16[2,96,4,5,128]{4,1,3,0,2:T(8,128)(2,1)S(1)} %get-tuple-element.683), kind=kOutput, calls=%fused_computation.26.clone.1 | convolution fusion | flops 509210880 | bytes 9388032 | tf_op jit(solution)/shard_map/while/body/eval_jaxpr/crhgd,nhd->chgrn/dot_general | solution.py:22
  166.4 4.4 %fusion.61 = f32[2,4,5,96]{3,2,0,1:T(8,128)S(1)} fusion(f32[4,512,2,96,5]{1,3,4,2,0:T(8,128)} %get-tuple-element.646, f32[2,4,5,96]{3,2,0,1:T(8,128)S(1)} %select_maximum_fusion.2, pred[2,512]{1,0:T(4,128)(4,1)S(1)} %broadcast_compare_fusion.9), kind=kLoop, calls=%fused_computation.25.clone.1 | loop fusion | flops 7860480 | bytes 7896064 | tf_op jit(solution)/shard_map/while/body/eval_jaxpr/reduce_sum | solution.py:36
  171.1 5.9 %bitcast_add_fusion.2 = f32[2,4,5,96,128]{4,3,2,0,1:T(8,128)} fusion(f32[2,4,5,96,128]{4,3,2,0,1:T(8,128)} %get-tuple-element.666, bf16[512,4,128,1,1]{0,2,4,3,1:T(8,128)(2,1)S(1)} %bitcast.91, f32[4,512,2,96,5]{1,3,4,2,0:T(8,128)} %get-tuple-element.646, f32[2,4,5,96]{3,2,0,1:T(8,128)S(1)} %select_maximum_fusion.2, ...), kind=kOutput, calls=%fused_computation.32.clone.1 | convolution fusion | flops 512655360 | bytes 12352513 | tf_op jit(solution)/shard_map/while/body/eval_jaxpr/chgrn,nhd->chgrd/dot_general | solution.py:38
  178.6 4.2 %fusion.60 = (f32[2,4,5,96]{3,2,0,1:T(8,128)S(1)}, f32[4,512,2,96,5]{1,3,4,2,0:T(8,128)}) fusion(pred[2,512]{1,0:T(4,128)(4,1)S(1)} %broadcast_compare_fusion.9, bf16[512,4,128,1,1]{0,2,4,3,1:T(8,128)(2,1)S(1)} %bitcast.88, bf16[2,96,4,5,128]{4,1,3,0,2:T(8,128)(2,1)S(1)} %get-tuple-element.683), kind=kOutput, calls=%fused_computation.26.clone.1 | convolution fusion | flops 509210880 | bytes 9388032 | tf_op jit(solution)/shard_map/while/body/eval_jaxpr/crhgd,nhd->chgrn/dot_general | solution.py:22
  182.8 4.4 %fusion.61 = f32[2,4,5,96]{3,2,0,1:T(8,128)S(1)} fusion(f32[4,512,2,96,5]{1,3,4,2,0:T(8,128)} %get-tuple-element.646, f32[2,4,5,96]{3,2,0,1:T(8,128)S(1)} %select_maximum_fusion.2, pred[2,512]{1,0:T(4,128)(4,1)S(1)} %broadcast_compare_fusion.9), kind=kLoop, calls=%fused_computation.25.clone.1 | loop fusion | flops 7860480 | bytes 7896064 | tf_op jit(solution)/shard_map/while/body/eval_jaxpr/reduce_sum | solution.py:36
  187.5 5.9 %bitcast_add_fusion.2 = f32[2,4,5,96,128]{4,3,2,0,1:T(8,128)} fusion(f32[2,4,5,96,128]{4,3,2,0,1:T(8,128)} %get-tuple-element.666, bf16[512,4,128,1,1]{0,2,4,3,1:T(8,128)(2,1)S(1)} %bitcast.91, f32[4,512,2,96,5]{1,3,4,2,0:T(8,128)} %get-tuple-element.646, f32[2,4,5,96]{3,2,0,1:T(8,128)S(1)} %select_maximum_fusion.2, ...), kind=kOutput, calls=%fused_computation.32.clone.1 | convolution fusion | flops 512655360 | bytes 12352513 | tf_op jit(solution)/shard_map/while/body/eval_jaxpr/chgrn,nhd->chgrd/dot_general | solution.py:38
  196.3 22.1 %all-gather.12.cloned.1.call-done = bf16[2,768,512]{2,0,1:T(2,128)(2,1)} async-done(((bf16[2,96,512]{2,0,1:T(2,128)(2,1)}), bf16[2,768,512]{2,0,1:T(2,128)(2,1)}) %all-gather.12.cloned.1.call-update) | async-done | bytes 1572880 | tf_op jit(solution)/shard_map/all_gather | solution.py:120
  218.4 41.8 %while.36 = (s32[]{:T(128)}, f32[2,4,5,96]{3,2,1,0:T(8,128)}, f32[2,4,5,96]{3,2,1,0:T(8,128)}, f32[2,4,5,96,128]{4,3,2,1,0:T(8,128)S(1)}, s32[768]{0:T(1024)S(1)...) while((s32[]{:T(128)}, f32[2,4,5,96]{3,2,1,0:T(8,128)}, ...), condition=%wide.region_7.8_spmd.clone, body=%wide.region_4.7_spmd.clone.sunk | while | flops 515194976 | bytes 38561872 | solution.py:65
  219.3 1.9 constant_dynamic-slice_fusion.8
  221.8 2.2 fusion.54
  224.0 1.8 copy-done
  228.0 3.7 %multiply_add_fusion.5 = f32[2,4,5,96,128]{4,3,2,1,0:T(8,128)S(1)} fusion(f32[2,4,5,96,128]{4,3,2,1,0:T(8,128)S(1)} %get-tuple-element.706, bf16[2,256,4,128,1]{1,3,4,2,0:T(8,128)(2,1)S(1)} %bitcast.89, f32[2,4,256,96,5]{2,3,4,1,0:T(8,128)} %copy-done, f32[2,4,5,96]{3,2,1,0:T(8,128)S(1)} %max.19, pred[2,96,256]{2,1,0:T(8,128)(4,1)S(1)} %copy-done.1, ...), kind=kOutput, calls=%fused_computation.7.clone.1 | convolution fusion | flops 256573440 | bytes 8468480 | tf_op jit(solution)/shard_map/while/body/eval_jaxpr/chgrn,cnhd->chgrd/dot_general | solution.py:42
  233.2 1.9 constant_dynamic-slice_fusion.8
  235.7 2.2 fusion.54
  238.0 1.8 copy-done
  241.9 3.7 %multiply_add_fusion.5 = f32[2,4,5,96,128]{4,3,2,1,0:T(8,128)S(1)} fusion(f32[2,4,5,96,128]{4,3,2,1,0:T(8,128)S(1)} %get-tuple-element.706, bf16[2,256,4,128,1]{1,3,4,2,0:T(8,128)(2,1)S(1)} %bitcast.89, f32[2,4,256,96,5]{2,3,4,1,0:T(8,128)} %copy-done, f32[2,4,5,96]{3,2,1,0:T(8,128)S(1)} %max.19, pred[2,96,256]{2,1,0:T(8,128)(4,1)S(1)} %copy-done.1, ...), kind=kOutput, calls=%fused_computation.7.clone.1 | convolution fusion | flops 256573440 | bytes 8468480 | tf_op jit(solution)/shard_map/while/body/eval_jaxpr/chgrn,cnhd->chgrd/dot_general | solution.py:42
  247.2 1.9 constant_dynamic-slice_fusion.8
  249.7 2.2 fusion.54
  251.9 1.8 copy-done
  255.9 3.7 %multiply_add_fusion.5 = f32[2,4,5,96,128]{4,3,2,1,0:T(8,128)S(1)} fusion(f32[2,4,5,96,128]{4,3,2,1,0:T(8,128)S(1)} %get-tuple-element.706, bf16[2,256,4,128,1]{1,3,4,2,0:T(8,128)(2,1)S(1)} %bitcast.89, f32[2,4,256,96,5]{2,3,4,1,0:T(8,128)} %copy-done, f32[2,4,5,96]{3,2,1,0:T(8,128)S(1)} %max.19, pred[2,96,256]{2,1,0:T(8,128)(4,1)S(1)} %copy-done.1, ...), kind=kOutput, calls=%fused_computation.7.clone.1 | convolution fusion | flops 256573440 | bytes 8468480 | tf_op jit(solution)/shard_map/while/body/eval_jaxpr/chgrn,cnhd->chgrd/dot_general | solution.py:42
  268.5 27.6 %all-gather.14.cloned.1.call-done = bf16[8,96,2560]{2,1,0:T(8,128)(2,1)} async-done(((bf16[2,96,2560]{2,1,0:T(8,128)(2,1)}), bf16[8,96,2560]{2,1,0:T(8,128)(2,1)}) %all-gather.14.cloned.1.call-update) | async-done | bytes 3932176 | tf_op jit(solution)/shard_map/all_gather | solution.py:135
  (131 shorter events, 35.4 us)
Async XLA Ops:
  6.5 63.1 %all-gather.6.cloned.1.call-start = ((), (), s32[]{:S(2)}) async-start(), calls=%async_computation | async-start | bytes 2162688 | tf_op jit(solution)/shard_map/all_gather | solution.py:90
  7.3 120.7 %all-gather.8.cloned.1.call-start = ((), (), s32[]{:S(2)}) async-start(), calls=%async_computation.1 | async-start | bytes 2162688 | tf_op jit(solution)/shard_map/all_gather | solution.py:91
  8.0 188.3 %all-gather.10.cloned.1.call-start = ((), (), s32[]{:S(2)}) async-start(), calls=%async_computation.2 | async-start | bytes 1769472 | tf_op jit(solution)/shard_map/all_gather | solution.py:119
  9.9 5.8 %copy-start.6 = (s32[8]{0:T(128)S(1)}, s32[8]{0:T(128)}, u32[]{:S(2)}) copy-start(s32[8]{0:T(128)} %param.18) | copy-start | bytes 100
  9.9 5.9 %copy-start.7 = (s32[8]{0:T(128)S(1)}, s32[8]{0:T(128)}, u32[]{:S(2)}) copy-start(s32[8]{0:T(128)} %param.17) | copy-start | bytes 100
  9.9 208.5 %all-gather.12.cloned.1.call-start = ((), (), s32[]{:S(2)}) async-start(), calls=%async_computation.3 | async-start | bytes 1769472 | tf_op jit(solution)/shard_map/all_gather | solution.py:120
  11.8 284.3 %all-gather.14.cloned.1.call-start = ((), (), s32[]{:S(2)}) async-start(), calls=%async_computation.4 | async-start | bytes 4915200 | tf_op jit(solution)/shard_map/all_gather | solution.py:135
  221.8 2.2 copy-start.2
  221.8 4.1 %copy-start.1 = (pred[2,96,256]{2,1,0:T(8,128)(4,1)S(1)}, pred[2,96,256]{2,1,0:T(8,128)(4,1)}, u32[]{:S(2)}) copy-start(pred[2,96,256]{2,1,0:T(8,128)(4,1)} %broadcast_and_fusion.2) | copy-start | bytes 147460 | tf_op jit(solution)/shard_map/while
  221.8 5.6 %copy-start.3 = (f32[2,4,5,96]{3,2,1,0:T(8,128)S(1)}, f32[2,4,5,96]{3,2,1,0:T(8,128)}, u32[]{:S(2)}) copy-start(f32[2,4,5,96]{3,2,1,0:T(8,128)} %get-tuple-element.705) | copy-start | bytes 46084 | tf_op jit(solution)/shard_map/while
  224.0 1.8 copy-start
  227.4 4.3 %copy-start.4 = (f32[2,4,5,96]{3,2,1,0:T(8,128)}, f32[2,4,5,96]{3,2,1,0:T(8,128)S(1)}, u32[]{:S(2)}) copy-start(f32[2,4,5,96]{3,2,1,0:T(8,128)S(1)} %get-tuple-element.719) | copy-start | bytes 46084 | tf_op jit(solution)/shard_map/while
  235.7 2.2 copy-start.2
  235.7 4.1 %copy-start.1 = (pred[2,96,256]{2,1,0:T(8,128)(4,1)S(1)}, pred[2,96,256]{2,1,0:T(8,128)(4,1)}, u32[]{:S(2)}) copy-start(pred[2,96,256]{2,1,0:T(8,128)(4,1)} %broadcast_and_fusion.2) | copy-start | bytes 147460 | tf_op jit(solution)/shard_map/while
  235.7 5.6 %copy-start.3 = (f32[2,4,5,96]{3,2,1,0:T(8,128)S(1)}, f32[2,4,5,96]{3,2,1,0:T(8,128)}, u32[]{:S(2)}) copy-start(f32[2,4,5,96]{3,2,1,0:T(8,128)} %get-tuple-element.705) | copy-start | bytes 46084 | tf_op jit(solution)/shard_map/while
  237.9 1.8 copy-start
  241.4 4.3 %copy-start.4 = (f32[2,4,5,96]{3,2,1,0:T(8,128)}, f32[2,4,5,96]{3,2,1,0:T(8,128)S(1)}, u32[]{:S(2)}) copy-start(f32[2,4,5,96]{3,2,1,0:T(8,128)S(1)} %get-tuple-element.719) | copy-start | bytes 46084 | tf_op jit(solution)/shard_map/while
  249.6 2.2 copy-start.2
  249.6 4.1 %copy-start.1 = (pred[2,96,256]{2,1,0:T(8,128)(4,1)S(1)}, pred[2,96,256]{2,1,0:T(8,128)(4,1)}, u32[]{:S(2)}) copy-start(pred[2,96,256]{2,1,0:T(8,128)(4,1)} %broadcast_and_fusion.2) | copy-start | bytes 147460 | tf_op jit(solution)/shard_map/while
  249.7 5.6 %copy-start.3 = (f32[2,4,5,96]{3,2,1,0:T(8,128)S(1)}, f32[2,4,5,96]{3,2,1,0:T(8,128)}, u32[]{:S(2)}) copy-start(f32[2,4,5,96]{3,2,1,0:T(8,128)} %get-tuple-element.705) | copy-start | bytes 46084 | tf_op jit(solution)/shard_map/while
  251.9 1.8 copy-start
  255.3 4.3 %copy-start.4 = (f32[2,4,5,96]{3,2,1,0:T(8,128)}, f32[2,4,5,96]{3,2,1,0:T(8,128)S(1)}, u32[]{:S(2)}) copy-start(f32[2,4,5,96]{3,2,1,0:T(8,128)S(1)} %get-tuple-element.719) | copy-start | bytes 46084 | tf_op jit(solution)/shard_map/while
  261.5 2.6 copy-start.5
Sparse Core Ops, SparseCore 0:
  10.3 59.2 all-gather.5
  72.6 55.3 all-gather.7
  130.2 43.0 all-gather.9
  175.3 43.0 all-gather.11
  264.3 31.7 all-gather.13
where the time goes:
time: 306 us; the launch traced here: 305 us
  waiting for transfers between devices  163 us (53%)
  matrix products  57.7 us (19%)
  local copies, waits for them, and re-layouts  36.7 us (12%)
  other arithmetic  29.6 us (10%)
  between operations  16.9 us (6%)
    all_gather x1, waiting for transfers between devices, body(): lax.all_gather(prompt_value_array, ('cand', 'seq'), axis=0, tiled=True)  58.4 us
    all_gather x1, waiting for transfers between devices, body(): lax.all_gather(prompt_key_array, ('cand', 'seq'), axis=0, tiled=True)  53.7 us
    all_gather x1, waiting for transfers between devices, body(): gathered = lax.all_gather(attended, 'cand', axis=0, tiled=True)  27.6 us
    dot_general x4, matrix products, attend_block(): jnp.einsum('chgrn,nhd->chgrd', weights, values_split, preferred_element_t...  23.1 us
    reduce_sum x7, other arithmetic, attend_block(): new_total = running_total * rescale + jnp.sum(exponent, axis=-1)  22.3 us
    all_gather x1, waiting for transfers between devices, body(): lax.all_gather(response_value_array, 'seq', axis=1, tiled=True)  22.1 us
    dot_general x4, matrix products, attend_block(): jnp.einsum('crhgd,nhd->chgrn', query_rows, keys_split, preferred_element_...  16.9 us
    dynamic_slice x14, local copies, waits for them, and re-layouts, one_block(): lax.dynamic_slice_in_dim(all_values, block_start, block_len, keys_axis)  13.3 us
  transfers between devices with their start and end apart: 5, of which 4 were waited for; matrix products, arithmetic and copies ran while one was open for 25% of the time, Pallas kernels for 0%

commit v1 on v0

--- a/solution.py
+++ b/solution.py
@@ -115,9 +115,29 @@
         allowed_of,
         True,
     )
+
+    def mix_sample(u_in):
+        fan = lax.axis_size("seq")
+        history = []
+        for p in range(fan):
+            history.append((p, (p + 1) % fan))
+        seen = []
+        for p in range(fan):
+            seen.append((p, (p - 1) % fan))
+        part_now, big = ([u_in], [u_in])
+        for _ in range(fan // 2):
+            e_next = lax.ppermute(part_now[-1], "seq", history)
+            part_now.append(e_next)
+        for _ in range((fan - 1) // 2):
+            right_arr = lax.ppermute(big[-1], "seq", seen)
+            big.append(right_arr)
+        h_now = jnp.concatenate([*part_now[::-1], *big[1:]], axis=1)
+        newest = jnp.roll(h_now, (lax.axis_index("seq") - fan // 2) * u_in.shape[1], axis=1)
+        return newest
+
     pieces = (
         lax.all_gather(response_key_array, "seq", axis=1, tiled=True),
-        lax.all_gather(response_value_array, "seq", axis=1, tiled=True),
+        mix_sample(response_value_array),
     )
     key_pos = jnp.arange(pieces[0].shape[1], dtype=jnp.int32)
 

time: 306 us -> 275 us (0.90)
  waiting for transfers between devices: 163 us -> 121 us
  starting transfers between devices: 0.16 us -> 18.8 us
  matrix products: 57.7 us -> 52.5 us
    all_gather x1, waiting for transfers between devices: 53.7 us -> 6.49 us  [body(): lax.all_gather(prompt_key_array, ('cand', 'seq'), axis=0, tiled=True)]
    ppermute x0 -> x7, waiting for transfers between devices: none -> 26.4 us  [the longest x4 20.8 us: mix_sample(): e_next = lax.ppermute(part_now[-1], 'seq', history)]
    all_gather x1 -> x0, waiting for transfers between devices: 22.1 us -> none  [body(): lax.all_gather(response_value_array, 'seq', axis=1, tiled=True)]
    ppermute x0 -> x7, starting transfers between devices: none -> 18.7 us  [the longest x3 10.7 us: mix_sample(): right_arr = lax.ppermute(big[-1], 'seq', seen)]
    while x37 -> x7, local copies, waits for them, and re-layouts: 7.33 us -> 0.03 us
    concatenate x0 -> x1, local copies, waits for them, and re-layouts: none -> 6.14 us  [mix_sample(): jnp.roll(h_now, (lax.axis_index('seq') - fan // 2) * u_in.shape[1], axis=1)]
    dot_general x3, matrix products: 11.1 us -> 6.01 us  [attend_block(): jnp.einsum('chgrn,cnhd->chgrd', weights, values_split, preferred_element_...]
    dynamic_slice x7 -> x10, local copies, waits for them, and re-layouts: 2.48 us -> 6.71 us  [one_block(): lax.dynamic_slice_in_dim(all_keys, block_start, block_len, keys_axis)]
  transfers between devices with their start and end apart: 5 -> 11, of which waited for: 4 -> 8; matrix products, arithmetic and copies ran while one was open for 25% -> 31% of each run, Pallas kernels for 0% -> 0%
where the time goes in v1:
time: 275 us; the launch traced here: 273 us
  waiting for transfers between devices  121 us (44%)
  matrix products  52.5 us (19%)
  local copies, waits for them, and re-layouts  37.1 us (13%)
  other arithmetic  27 us (10%)
  starting transfers between devices  18.8 us (7%)
  between operations  16.9 us (6%)
    all_gather x1, waiting for transfers between devices, body(): lax.all_gather(prompt_value_array, ('cand', 'seq'), axis=0, tiled=True)  58.4 us
    all_gather x1, waiting for transfers between devices, body(): gathered = lax.all_gather(attended, 'cand', axis=0, tiled=True)  27.9 us
    dot_general x4, matrix products, attend_block(): jnp.einsum('chgrn,nhd->chgrd', weights, values_split, preferred_element_t...  23.1 us
    reduce_sum x7, other arithmetic, attend_block(): new_total = running_total * rescale + jnp.sum(exponent, axis=-1)  22.4 us
    ppermute x4, waiting for transfers between devices, mix_sample(): e_next = lax.ppermute(part_now[-1], 'seq', history)  20.8 us
    dot_general x4, matrix products, attend_block(): jnp.einsum('crhgd,nhd->chgrn', query_rows, keys_split, preferred_element_...  16.9 us
    ppermute x3, starting transfers between devices, mix_sample(): right_arr = lax.ppermute(big[-1], 'seq', seen)  10.7 us
    dynamic_slice x11, local copies, waits for them, and re-layouts, one_block(): lax.dynamic_slice_in_dim(all_values, block_start, block_len, keys_axis)  9.17 us
  transfers between devices with their start and end apart: 11, of which 8 were waited for; matrix products, arithmetic and copies ran while one was open for 31% of the time, Pallas kernels for 0%

profile of v1, /device:TPU:0, one launch (start us, length us, event | category | flops | bytes accessed | tf_op | source)
XLA Modules:
  0.0 273.4 jit_solution(17922067550043073710)
XLA Ops:
  9.2 3.0 %collective-permute-start = (bf16[2,96,512]{1,2,0:T(8,128)(2,1)S(1)}, bf16[2,96,512]{1,2,0:T(8,128)(2,1)S(1)}, u32[]{:S(2)}, u32[]{:S(2)}) collective-permute-start(bf16[2,96,512]{1,2,0:T(8,128)(2,1)S(1)} %copy.62), channel_id=1, source_target_pairs={{0,1},{1,2},{2,3},{3,4},{4,5},{5,6},{6,7},{7,0},{8,9},{9,10},{10,1... | collective-permute-start | bytes 589832 | tf_op jit(solution)/shard_map/ppermute | solution.py:129
  12.2 3.1 %collective-permute-start.4 = (bf16[2,96,512]{1,2,0:T(8,128)(2,1)S(1)}, bf16[2,96,512]{1,2,0:T(8,128)(2,1)S(1)}, u32[]{:S(2)}, u32[]{:S(2)}) collective-permute-start(bf16[2,96,512]{1,2,0:T(8,128)(2,1)S(1)} %copy.62), channel_id=1, source_target_pairs={{0,7},{1,0},{2,1},{3,2},{4,3},{5,4},{6,5},{7,6},{8,15},{9,8},{10,9... | collective-permute-start | bytes 589832 | tf_op jit(solution)/shard_map/ppermute | solution.py:132
  15.3 8.5 %collective-permute-done = bf16[2,96,512]{1,2,0:T(8,128)(2,1)S(1)} collective-permute-done((bf16[2,96,512]{1,2,0:T(8,128)(2,1)S(1)}, bf16[2,96,512]{1,2,0:T(8,128)(2,1)S(1)}, u32[]{:S(2)}, u32[]{:S(2)}) %collective-permute-start) | collective-permute-done | bytes 196640 | tf_op jit(solution)/shard_map/ppermute | solution.py:129
  23.8 2.5 collective-permute-start.1
  26.3 3.0 %collective-permute-start.5 = (bf16[2,96,512]{1,2,0:T(8,128)(2,1)S(1)}, bf16[2,96,512]{1,2,0:T(8,128)(2,1)}, u32[]{:S(2)}, u32[]{:S(2)}) collective-permute-start(bf16[2,96,512]{1,2,0:T(8,128)(2,1)S(1)} %collective-permute-done.4), channel_id=1, source_target_pairs={{0,7},{1,0},{2,1},{3,2},{4,3},{5,4},{6,5},{7,6},{8,15},{9,8},{10,9... | collective-permute-start | bytes 589832 | tf_op jit(solution)/shard_map/ppermute | solution.py:132
  29.4 7.5 %collective-permute-done.1 = bf16[2,96,512]{1,2,0:T(8,128)(2,1)S(1)} collective-permute-done((bf16[2,96,512]{1,2,0:T(8,128)(2,1)S(1)}, bf16[2,96,512]{1,2,0:T(8,128)(2,1)S(1)}, u32[]{:S(2)}, u32[]{:S(2)}) %collective-permute-start.1) | collective-permute-done | bytes 196640 | tf_op jit(solution)/shard_map/ppermute | solution.py:129
  36.9 2.5 collective-permute-start.2
  45.2 4.6 %collective-permute-start.6 = (bf16[2,96,512]{1,2,0:T(8,128)(2,1)}, bf16[2,96,512]{1,2,0:T(8,128)(2,1)S(1)}, u32[]{:S(2)}, u32[]{:S(2)}) collective-permute-start(bf16[2,96,512]{1,2,0:T(8,128)(2,1)} %collective-permute-done.5), channel_id=1, source_target_pairs={{0,7},{1,0},{2,1},{3,2},{4,3},{5,4},{6,5},{7,6},{8,15},{9,8},{10,9... | collective-permute-start | bytes 589832 | tf_op jit(solution)/shard_map/ppermute | solution.py:132
  50.0 5.6 %collective-permute-done.6 = bf16[2,96,512]{1,2,0:T(8,128)(2,1)S(1)} collective-permute-done((bf16[2,96,512]{1,2,0:T(8,128)(2,1)}, bf16[2,96,512]{1,2,0:T(8,128)(2,1)S(1)}, u32[]{:S(2)}, u32[]{:S(2)}) %collective-permute-start.6) | collective-permute-done | bytes 196640 | tf_op jit(solution)/shard_map/ppermute | solution.py:132
  55.6 4.6 %collective-permute-done.3 = bf16[2,96,512]{1,2,0:T(8,128)(2,1)S(1)} collective-permute-done((bf16[2,96,512]{1,2,0:T(8,128)(2,1)}, bf16[2,96,512]{1,2,0:T(8,128)(2,1)S(1)}, u32[]{:S(2)}, u32[]{:S(2)}) %collective-permute-start.3) | collective-permute-done | bytes 196640 | tf_op jit(solution)/shard_map/ppermute | solution.py:129
  60.2 6.1 %concatenate.6 = bf16[2,1536,512]{1,2,0:T(8,128)(2,1)} concatenate(bf16[2,96,512]{1,2,0:T(8,128)(2,1)S(1)} %collective-permute-done.3, bf16[2,96,512]{1,2,0:T(8,128)(2,1)} %collective-permute-done.2, bf16[2,96,512]{1,2,0:T(8,128)(2,1)S(1)} %collective-permute-done.1, bf16[2,96,512]{1,2,0:T(8,128)(2,1)S(1)} %collective-permute-done, bf16[2,96,512]{1,2,0:T(8,128)(2,1)S(1)} %copy.62, ...), dimensions={1} | concatenate | bytes 6291456 | tf_op jit(solution)/shard_map/jit(_roll_dynamic)/concatenate | solution.py:135
  66.3 3.4 %constant_dynamic-slice_fusion.6 = bf16[2,768,512]{1,2,0:T(8,128)(2,1)} fusion(bf16[2,1536,512]{1,2,0:T(8,128)(2,1)} %concatenate.6, s32[]{:T(128)S(6)} %select_n.71), kind=kLoop, calls=%fused_computation.50 | loop fusion | bytes 3145732 | tf_op jit(solution)/shard_map/jit(_roll_dynamic)/dynamic_slice | solution.py:135
  69.7 6.5 %all-gather.5.cloned.1.call-done = bf16[2048,512]{1,0:T(8,128)(2,1)} async-done(((bf16[64,512]{1,0:T(8,128)(2,1)}), bf16[2048,512]{1,0:T(8,128)(2,1)}) %all-gather.5.cloned.1.call-update) | async-done | bytes 2097168 | tf_op jit(solution)/shard_map/all_gather | solution.py:90
  76.2 58.4 %all-gather.7.cloned.1.call-done = bf16[2048,512]{1,0:T(8,128)(2,1)} async-done(((bf16[64,512]{1,0:T(8,128)(2,1)}), bf16[2048,512]{1,0:T(8,128)(2,1)}) %all-gather.7.cloned.1.call-update) | async-done | bytes 2097168 | tf_op jit(solution)/shard_map/all_gather | solution.py:91
  134.6 65.4 %while.37 = (s32[]{:T(128)}, f32[2,4,5,96]{3,2,0,1:T(8,128)S(1)}, f32[2,4,5,96]{3,2,0,1:T(8,128)S(1)}, f32[2,4,5,96,128]{4,3,2,0,1:T(8,128)}, s32[2048]{0:T(1024...) while((s32[]{:T(128)}, f32[2,4,5,96]{3,2,0,1:T(8,128)S(1)}, ...), condition=%wide.region_3.4_spmd.clone, body=%wide.region_0.3_spmd.clone.sunk | while | flops 1029754624 | bytes 34007244 | solution.py:65
  136.2 4.2 %fusion.60 = (f32[2,4,5,96]{3,2,0,1:T(8,128)S(1)}, f32[4,512,2,96,5]{1,3,4,2,0:T(8,128)}) fusion(pred[2,512]{1,0:T(4,128)(4,1)S(1)} %broadcast_compare_fusion.9, bf16[512,4,128,1,1]{0,2,4,3,1:T(8,128)(2,1)S(1)} %bitcast.88, bf16[2,96,4,5,128]{4,1,3,0,2:T(8,128)(2,1)S(1)} %get-tuple-element.677), kind=kOutput, calls=%fused_computation.26.clone.1 | convolution fusion | flops 509210880 | bytes 9388032 | tf_op jit(solution)/shard_map/while/body/eval_jaxpr/crhgd,nhd->chgrn/dot_general | solution.py:22
  140.5 4.5 %fusion.61 = f32[2,4,5,96]{3,2,0,1:T(8,128)S(1)} fusion(f32[4,512,2,96,5]{1,3,4,2,0:T(8,128)} %get-tuple-element.640, f32[2,4,5,96]{3,2,0,1:T(8,128)S(1)} %select_maximum_fusion.2, pred[2,512]{1,0:T(4,128)(4,1)S(1)} %broadcast_compare_fusion.9), kind=kLoop, calls=%fused_computation.25.clone.1 | loop fusion | flops 7860480 | bytes 7896064 | tf_op jit(solution)/shard_map/while/body/eval_jaxpr/reduce_sum | solution.py:36
  145.2 5.4 %bitcast_add_fusion.2 = f32[2,4,5,96,128]{4,3,2,0,1:T(8,128)} fusion(f32[2,4,5,96,128]{4,3,2,0,1:T(8,128)} %get-tuple-element.660, bf16[512,4,128,1,1]{0,2,4,3,1:T(8,128)(2,1)S(1)} %bitcast.91, f32[4,512,2,96,5]{1,3,4,2,0:T(8,128)} %get-tuple-element.640, f32[2,4,5,96]{3,2,0,1:T(8,128)S(1)} %select_maximum_fusion.2, ...), kind=kOutput, calls=%fused_computation.32.clone.1 | convolution fusion | flops 512655360 | bytes 12352513 | tf_op jit(solution)/shard_map/while/body/eval_jaxpr/chgrn,nhd->chgrd/dot_general | solution.py:38
  152.3 4.2 %fusion.60 = (f32[2,4,5,96]{3,2,0,1:T(8,128)S(1)}, f32[4,512,2,96,5]{1,3,4,2,0:T(8,128)}) fusion(pred[2,512]{1,0:T(4,128)(4,1)S(1)} %broadcast_compare_fusion.9, bf16[512,4,128,1,1]{0,2,4,3,1:T(8,128)(2,1)S(1)} %bitcast.88, bf16[2,96,4,5,128]{4,1,3,0,2:T(8,128)(2,1)S(1)} %get-tuple-element.677), kind=kOutput, calls=%fused_computation.26.clone.1 | convolution fusion | flops 509210880 | bytes 9388032 | tf_op jit(solution)/shard_map/while/body/eval_jaxpr/crhgd,nhd->chgrn/dot_general | solution.py:22
  156.5 4.4 %fusion.61 = f32[2,4,5,96]{3,2,0,1:T(8,128)S(1)} fusion(f32[4,512,2,96,5]{1,3,4,2,0:T(8,128)} %get-tuple-element.640, f32[2,4,5,96]{3,2,0,1:T(8,128)S(1)} %select_maximum_fusion.2, pred[2,512]{1,0:T(4,128)(4,1)S(1)} %broadcast_compare_fusion.9), kind=kLoop, calls=%fused_computation.25.clone.1 | loop fusion | flops 7860480 | bytes 7896064 | tf_op jit(solution)/shard_map/while/body/eval_jaxpr/reduce_sum | solution.py:36
  161.2 6.0 %bitcast_add_fusion.2 = f32[2,4,5,96,128]{4,3,2,0,1:T(8,128)} fusion(f32[2,4,5,96,128]{4,3,2,0,1:T(8,128)} %get-tuple-element.660, bf16[512,4,128,1,1]{0,2,4,3,1:T(8,128)(2,1)S(1)} %bitcast.91, f32[4,512,2,96,5]{1,3,4,2,0:T(8,128)} %get-tuple-element.640, f32[2,4,5,96]{3,2,0,1:T(8,128)S(1)} %select_maximum_fusion.2, ...), kind=kOutput, calls=%fused_computation.32.clone.1 | convolution fusion | flops 512655360 | bytes 12352513 | tf_op jit(solution)/shard_map/while/body/eval_jaxpr/chgrn,nhd->chgrd/dot_general | solution.py:38
  168.8 4.2 %fusion.60 = (f32[2,4,5,96]{3,2,0,1:T(8,128)S(1)}, f32[4,512,2,96,5]{1,3,4,2,0:T(8,128)}) fusion(pred[2,512]{1,0:T(4,128)(4,1)S(1)} %broadcast_compare_fusion.9, bf16[512,4,128,1,1]{0,2,4,3,1:T(8,128)(2,1)S(1)} %bitcast.88, bf16[2,96,4,5,128]{4,1,3,0,2:T(8,128)(2,1)S(1)} %get-tuple-element.677), kind=kOutput, calls=%fused_computation.26.clone.1 | convolution fusion | flops 509210880 | bytes 9388032 | tf_op jit(solution)/shard_map/while/body/eval_jaxpr/crhgd,nhd->chgrn/dot_general | solution.py:22
  173.0 4.4 %fusion.61 = f32[2,4,5,96]{3,2,0,1:T(8,128)S(1)} fusion(f32[4,512,2,96,5]{1,3,4,2,0:T(8,128)} %get-tuple-element.640, f32[2,4,5,96]{3,2,0,1:T(8,128)S(1)} %select_maximum_fusion.2, pred[2,512]{1,0:T(4,128)(4,1)S(1)} %broadcast_compare_fusion.9), kind=kLoop, calls=%fused_computation.25.clone.1 | loop fusion | flops 7860480 | bytes 7896064 | tf_op jit(solution)/shard_map/while/body/eval_jaxpr/reduce_sum | solution.py:36
  177.7 5.9 %bitcast_add_fusion.2 = f32[2,4,5,96,128]{4,3,2,0,1:T(8,128)} fusion(f32[2,4,5,96,128]{4,3,2,0,1:T(8,128)} %get-tuple-element.660, bf16[512,4,128,1,1]{0,2,4,3,1:T(8,128)(2,1)S(1)} %bitcast.91, f32[4,512,2,96,5]{1,3,4,2,0:T(8,128)} %get-tuple-element.640, f32[2,4,5,96]{3,2,0,1:T(8,128)S(1)} %select_maximum_fusion.2, ...), kind=kOutput, calls=%fused_computation.32.clone.1 | convolution fusion | flops 512655360 | bytes 12352513 | tf_op jit(solution)/shard_map/while/body/eval_jaxpr/chgrn,nhd->chgrd/dot_general | solution.py:38
  185.2 4.2 %fusion.60 = (f32[2,4,5,96]{3,2,0,1:T(8,128)S(1)}, f32[4,512,2,96,5]{1,3,4,2,0:T(8,128)}) fusion(pred[2,512]{1,0:T(4,128)(4,1)S(1)} %broadcast_compare_fusion.9, bf16[512,4,128,1,1]{0,2,4,3,1:T(8,128)(2,1)S(1)} %bitcast.88, bf16[2,96,4,5,128]{4,1,3,0,2:T(8,128)(2,1)S(1)} %get-tuple-element.677), kind=kOutput, calls=%fused_computation.26.clone.1 | convolution fusion | flops 509210880 | bytes 9388032 | tf_op jit(solution)/shard_map/while/body/eval_jaxpr/crhgd,nhd->chgrn/dot_general | solution.py:22
  189.5 4.4 %fusion.61 = f32[2,4,5,96]{3,2,0,1:T(8,128)S(1)} fusion(f32[4,512,2,96,5]{1,3,4,2,0:T(8,128)} %get-tuple-element.640, f32[2,4,5,96]{3,2,0,1:T(8,128)S(1)} %select_maximum_fusion.2, pred[2,512]{1,0:T(4,128)(4,1)S(1)} %broadcast_compare_fusion.9), kind=kLoop, calls=%fused_computation.25.clone.1 | loop fusion | flops 7860480 | bytes 7896064 | tf_op jit(solution)/shard_map/while/body/eval_jaxpr/reduce_sum | solution.py:36
  194.1 5.9 %bitcast_add_fusion.2 = f32[2,4,5,96,128]{4,3,2,0,1:T(8,128)} fusion(f32[2,4,5,96,128]{4,3,2,0,1:T(8,128)} %get-tuple-element.660, bf16[512,4,128,1,1]{0,2,4,3,1:T(8,128)(2,1)S(1)} %bitcast.91, f32[4,512,2,96,5]{1,3,4,2,0:T(8,128)} %get-tuple-element.640, f32[2,4,5,96]{3,2,0,1:T(8,128)S(1)} %select_maximum_fusion.2, ...), kind=kOutput, calls=%fused_computation.32.clone.1 | convolution fusion | flops 512655360 | bytes 12352513 | tf_op jit(solution)/shard_map/while/body/eval_jaxpr/chgrn,nhd->chgrd/dot_general | solution.py:38
  201.8 27.5 %while.36 = (s32[]{:T(128)}, f32[2,4,5,96]{3,2,1,0:T(8,128)S(1)}, f32[2,4,5,96]{3,2,1,0:T(8,128)S(1)}, f32[2,4,5,96,128]{4,3,2,1,0:T(8,128)S(1)}, s32[768]{0:T(1...) while((s32[]{:T(128)}, f32[2,4,5,96]{3,2,1,0:T(8,128)S(1)}, ...), condition=%wide.region_7.8_spmd.clone, body=%wide.region_4.7_spmd.clone.sunk | while | flops 515194976 | bytes 21403604 | solution.py:65
  204.0 2.2 fusion.54
  213.2 2.2 fusion.54
  222.3 2.2 fusion.54
  236.7 27.9 %all-gather.11.cloned.1.call-done = bf16[8,96,2560]{2,1,0:T(8,128)(2,1)} async-done(((bf16[2,96,2560]{2,1,0:T(8,128)(2,1)}), bf16[8,96,2560]{2,1,0:T(8,128)(2,1)}) %all-gather.11.cloned.1.call-update) | async-done | bytes 3932176 | tf_op jit(solution)/shard_map/all_gather | solution.py:155
  (114 shorter events, 44.6 us)
Async XLA Ops:
  6.5 69.7 %all-gather.5.cloned.1.call-start = ((), (), s32[]{:S(2)}) async-start(), calls=%async_computation | async-start | bytes 2162688 | tf_op jit(solution)/shard_map/all_gather | solution.py:90
  7.3 127.3 %all-gather.7.cloned.1.call-start = ((), (), s32[]{:S(2)}) async-start(), calls=%async_computation.1 | async-start | bytes 2162688 | tf_op jit(solution)/shard_map/all_gather | solution.py:91
  8.0 37.0 %copy-start.1 = (s32[8]{0:T(128)S(1)}, s32[8]{0:T(128)}, u32[]{:S(2)}) copy-start(s32[8]{0:T(128)} %param.18) | copy-start | bytes 100
  8.0 37.1 %copy-start.2 = (s32[8]{0:T(128)S(1)}, s32[8]{0:T(128)}, u32[]{:S(2)}) copy-start(s32[8]{0:T(128)} %param.17) | copy-start | bytes 100
  8.0 193.7 %all-gather.9.cloned.1.call-start = ((), (), s32[]{:S(2)}) async-start(), calls=%async_computation.2 | async-start | bytes 1769472 | tf_op jit(solution)/shard_map/all_gather | solution.py:139
  9.2 14.7 %collective-permute-start = (bf16[2,96,512]{1,2,0:T(8,128)(2,1)S(1)}, bf16[2,96,512]{1,2,0:T(8,128)(2,1)S(1)}, u32[]{:S(2)}, u32[]{:S(2)}) collective-permute-start(bf16[2,96,512]{1,2,0:T(8,128)(2,1)S(1)} %copy.62), channel_id=1, source_target_pairs={{0,1},{1,2},{2,3},{3,4},{4,5},{5,6},{6,7},{7,0},{8,9},{9,10},{10,1... | collective-permute-start | bytes 589832 | tf_op jit(solution)/shard_map/ppermute | solution.py:129
  12.2 14.1 %collective-permute-start.4 = (bf16[2,96,512]{1,2,0:T(8,128)(2,1)S(1)}, bf16[2,96,512]{1,2,0:T(8,128)(2,1)S(1)}, u32[]{:S(2)}, u32[]{:S(2)}) collective-permute-start(bf16[2,96,512]{1,2,0:T(8,128)(2,1)S(1)} %copy.62), channel_id=1, source_target_pairs={{0,7},{1,0},{2,1},{3,2},{4,3},{5,4},{6,5},{7,6},{8,15},{9,8},{10,9... | collective-permute-start | bytes 589832 | tf_op jit(solution)/shard_map/ppermute | solution.py:132
  23.8 13.0 %collective-permute-start.1 = (bf16[2,96,512]{1,2,0:T(8,128)(2,1)S(1)}, bf16[2,96,512]{1,2,0:T(8,128)(2,1)S(1)}, u32[]{:S(2)}, u32[]{:S(2)}) collective-permute-start(bf16[2,96,512]{1,2,0:T(8,128)(2,1)S(1)} %collective-permute-done), channel_id=1, source_target_pairs={{0,1},{1,2},{2,3},{3,4},{4,5},{5,6},{6,7},{7,0},{8,9},{9,10},{10,1... | collective-permute-start | bytes 589832 | tf_op jit(solution)/shard_map/ppermute | solution.py:129
  26.3 18.9 %collective-permute-start.5 = (bf16[2,96,512]{1,2,0:T(8,128)(2,1)S(1)}, bf16[2,96,512]{1,2,0:T(8,128)(2,1)}, u32[]{:S(2)}, u32[]{:S(2)}) collective-permute-start(bf16[2,96,512]{1,2,0:T(8,128)(2,1)S(1)} %collective-permute-done.4), channel_id=1, source_target_pairs={{0,7},{1,0},{2,1},{3,2},{4,3},{5,4},{6,5},{7,6},{8,15},{9,8},{10,9... | collective-permute-start | bytes 589832 | tf_op jit(solution)/shard_map/ppermute | solution.py:132
  36.9 13.0 %collective-permute-start.2 = (bf16[2,96,512]{1,2,0:T(8,128)(2,1)S(1)}, bf16[2,96,512]{1,2,0:T(8,128)(2,1)}, u32[]{:S(2)}, u32[]{:S(2)}) collective-permute-start(bf16[2,96,512]{1,2,0:T(8,128)(2,1)S(1)} %collective-permute-done.1), channel_id=1, source_target_pairs={{0,1},{1,2},{2,3},{3,4},{4,5},{5,6},{6,7},{7,0},{8,9},{9,10},{10,1... | collective-permute-start | bytes 589832 | tf_op jit(solution)/shard_map/ppermute | solution.py:129
  41.2 223.4 %all-gather.11.cloned.1.call-start = ((), (), s32[]{:S(2)}) async-start(), calls=%async_computation.3 | async-start | bytes 4915200 | tf_op jit(solution)/shard_map/all_gather | solution.py:155
  45.2 10.4 %collective-permute-start.6 = (bf16[2,96,512]{1,2,0:T(8,128)(2,1)}, bf16[2,96,512]{1,2,0:T(8,128)(2,1)S(1)}, u32[]{:S(2)}, u32[]{:S(2)}) collective-permute-start(bf16[2,96,512]{1,2,0:T(8,128)(2,1)} %collective-permute-done.5), channel_id=1, source_target_pairs={{0,7},{1,0},{2,1},{3,2},{4,3},{5,4},{6,5},{7,6},{8,15},{9,8},{10,9... | collective-permute-start | bytes 589832 | tf_op jit(solution)/shard_map/ppermute | solution.py:132
  49.8 10.4 %collective-permute-start.3 = (bf16[2,96,512]{1,2,0:T(8,128)(2,1)}, bf16[2,96,512]{1,2,0:T(8,128)(2,1)S(1)}, u32[]{:S(2)}, u32[]{:S(2)}) collective-permute-start(bf16[2,96,512]{1,2,0:T(8,128)(2,1)} %collective-permute-done.2), channel_id=1, source_target_pairs={{0,1},{1,2},{2,3},{3,4},{4,5},{5,6},{6,7},{7,0},{8,9},{9,10},{10,1... | collective-permute-start | bytes 589832 | tf_op jit(solution)/shard_map/ppermute | solution.py:129
  229.8 2.6 copy-start
Sparse Core Ops, SparseCore 0:
  10.3 65.8 all-gather.4
  79.2 55.3 all-gather.6
  136.8 43.0 all-gather.8
  232.5 31.9 all-gather.10
